TPU v7x, 32 devices: a whole 2x2x4 slice. The times are simulated.
32 devices in a mesh: row: 8 (over y, x, core), col: 4 (over z).
Axes of the slice: x: 2, y: 2, z: 4, core: 2. Of those that a mesh axis runs over, the one named last changes fastest.
Arguments:
- upper_s: float32 [4, 2048, 8, 1024], P(None, 'row', None, 'col')
- upper_t: float32 [4, 2048, 8, 1024], P(None, 'row', None, 'col')
- left_vectors: float32 [4, 2048, 8, 1024], P(None, 'row', None, 'col'), may hold values from -6 to 6
- right_vectors: float32 [4, 2048, 8, 1024], P(None, 'row', None, 'col'), may hold values from -6 to 6
- window_starts: int32 [3, 16], replicated, may hold values from 0 to 31, as said below
- selection: int32 [3, 16, 256], replicated, may hold values 0 or 1
- window_factors: float32 [3, 16, 2, 256, 256], P(None, 'row')
Outputs:
- new_s: float32 [4, 2048, 8, 1024], P(None, 'row', None, 'col')
- new_t: float32 [4, 2048, 8, 1024], P(None, 'row', None, 'col')
- new_left: float32 [4, 2048, 8, 1024], P(None, 'row', None, 'col')
- new_right: float32 [4, 2048, 8, 1024], P(None, 'row', None, 'col')
Inputs may be any that keep to these rules, and one draw needn't show every extreme that they name: `window_starts`: within each round the 16 block numbers are distinct.
All inputs are finite; a program needn't handle non-finite values.
Results may differ from a plain program's by a relative error of at most 0.0001.
Values sent between devices are 32-bit elements; how exact they have to be, the bound alone decides.
No kernel may reach another device: no remote copies, remote signals or barrier semaphores. Data moves between devices by JAX's collectives and lax.ppermute only.
A program may use at most 192 MiB of HBM per device.

v0:
```python
import jax
import jax.numpy as jnp
from jax import lax
from jax.sharding import PartitionSpec as P


def destinations(flags):
    earlier = jnp.cumsum(flags) - flags
    chosen = jnp.sum(flags)
    position = jnp.arange(flags.shape[0], dtype=jnp.int32)
    return jnp.where(flags == 1, earlier, chosen + position - earlier)


def window_bases(factors, flags):
    target = destinations(flags)
    return (jnp.take(factors[0], target, axis=0), jnp.take(factors[1], target, axis=0))


def fill_identity(starts, blocks, chosen):
    covered = jnp.sum((blocks[:, None] == starts[None, :]).astype(jnp.float32), axis=1)
    order_w = chosen.shape[1]
    return chosen + (1.0 - covered)[:, None, None] * jnp.eye(order_w, dtype=jnp.float32)


def rows_update(factor, matrix):
    return jnp.einsum("aij,aibl->ajbl", factor, matrix, precision=lax.Precision.HIGHEST)


def cols_update(matrix, factor):
    return jnp.einsum("aibm,bml->aibl", matrix, factor, precision=lax.Precision.HIGHEST)


def slot_factors(own_factors, own_starts, own_flags, starts, row_blocks, col_blocks):
    left_own, right_own = jax.vmap(window_bases)(own_factors, own_flags)
    stacked = jnp.stack([left_own, right_own], axis=1)
    placing = (col_blocks[:, None] == own_starts[None, :]).astype(jnp.float32)
    slots = jnp.einsum("jw,wxab->jxab", placing, stacked, precision=lax.Precision.HIGHEST)
    received = lax.psum(slots, "row")
    picking = (row_blocks[:, None] == col_blocks[None, :]).astype(jnp.float32)
    row_part = jnp.einsum("kj,jab->kab", picking, received[:, 0], precision=lax.Precision.HIGHEST)
    row_sum = lax.psum(row_part, "col")
    left_rows = fill_identity(starts, row_blocks, row_sum)
    left_cols = fill_identity(starts, col_blocks, received[:, 0])
    right_cols = fill_identity(starts, col_blocks, received[:, 1])
    return (left_rows, left_cols, right_cols)


def shards(upper_s, upper_t, left_vectors, right_vectors, window_starts, selection, window_factors):
    row_index = lax.axis_index("row")
    col_index = lax.axis_index("col")
    row_count = lax.axis_size("row")
    col_count = lax.axis_size("col")
    local_rows = upper_s.shape[0]
    local_cols = upper_s.shape[2]
    round_count = window_starts.shape[0]
    own_count = window_factors.shape[1]
    row_blocks = jnp.arange(local_rows, dtype=jnp.int32) * row_count + row_index
    col_blocks = jnp.arange(local_cols, dtype=jnp.int32) * col_count + col_index
    for round_idx in range(round_count):
        starts = window_starts[round_idx]
        first = row_index * own_count
        own_starts = lax.dynamic_slice_in_dim(starts, first, own_count, 0)
        own_flags = lax.dynamic_slice_in_dim(selection[round_idx], first, own_count, 0)
        left_rows, left_cols, right_cols = slot_factors(
            window_factors[round_idx], own_starts, own_flags, starts, row_blocks, col_blocks
        )
        upper_s = cols_update(rows_update(left_rows, upper_s), right_cols)
        upper_t = cols_update(rows_update(left_rows, upper_t), right_cols)
        left_vectors = cols_update(left_vectors, left_cols)
        right_vectors = cols_update(right_vectors, right_cols)
    return (upper_s, upper_t, left_vectors, right_vectors)


def solution(mesh):
    return jax.shard_map(
        shards,
        mesh=mesh,
        in_specs=(
            P(None, "row", None, "col"),
            P(None, "row", None, "col"),
            P(None, "row", None, "col"),
            P(None, "row", None, "col"),
            P(),
            P(),
            P(None, "row", None, None, None),
        ),
        out_specs=(
            P(None, "row", None, "col"),
            P(None, "row", None, "col"),
            P(None, "row", None, "col"),
            P(None, "row", None, "col"),
        ),
        check_vma=False,
    )
```

profile of v0, /device:TPU:0, one launch (start us, length us, event | category | flops | bytes accessed | tf_op | source)
XLA Modules:
  0.0 584.6 jit_solution(2492521393092527794)
XLA Ops:
  12.0 6.4 %gather_fusion = f32[512,256]{1,0:T(8,128)} fusion(f32[2,256,256]{2,1,0:T(8,128)S(1)} %get-tuple-element.58, s32[512]{0:T(512)S(1)} %bitcast.239), kind=kCustom, calls=%fused_computation.clone | custom fusion | bytes 1052672 | tf_op jit(solution)/shard_map/vmap(jit(_take))/gather | solution.py:16
  18.4 6.4 %gather_fusion.1 = f32[512,256]{1,0:T(8,128)} fusion(f32[2,256,256]{2,1,0:T(8,128)S(1)} %get-tuple-element.59, s32[512]{0:T(512)S(1)} %bitcast.240), kind=kCustom, calls=%fused_computation.1.clone | custom fusion | bytes 1052672 | tf_op jit(solution)/shard_map/vmap(jit(_take))/gather | solution.py:16
  29.0 6.4 %gather_fusion.2 = f32[512,256]{1,0:T(8,128)} fusion(f32[2,256,256]{2,1,0:T(8,128)S(1)} %get-tuple-element.56, s32[512]{0:T(512)S(1)} %bitcast.243), kind=kCustom, calls=%fused_computation.2.clone | custom fusion | bytes 1052672 | tf_op jit(solution)/shard_map/vmap(jit(_take))/gather | solution.py:16
  35.3 6.4 %gather_fusion.3 = f32[512,256]{1,0:T(8,128)} fusion(f32[2,256,256]{2,1,0:T(8,128)S(1)} %get-tuple-element.57, s32[512]{0:T(512)S(1)} %bitcast.244), kind=kCustom, calls=%fused_computation.3.clone | custom fusion | bytes 1052672 | tf_op jit(solution)/shard_map/vmap(jit(_take))/gather | solution.py:16
  54.1 4.3 fusion.42
  58.4 4.3 fusion.46
  63.9 15.0 %fusion.50 = f32[8,2,256,256]{3,0,2,1:T(8,128)} fusion(f32[2,1,256,256]{3,0,2,1:T(2,128)S(1)} %get-tuple-element.68, f32[2,1,256,256]{3,0,2,1:T(2,128)S(1)} %get-tuple-element.67, s32[8]{0:T(128)S(1)} %multiply_add_fusion.16, s32[2]{0:T(128)S(1)} %fusion.102), kind=kOutput, calls=%fused_computation.66 | convolution fusion | flops 25427984 | bytes 5242920 | tf_op jit(solution)/shard_map/jw,wxab->jxab/dot_general | solution.py:37
  79.4 174.4 %all-reduce.5.cloned.1.call-done = (f32[8,2,256,256]{3,0,2,1:T(8,128)}, f32[8,2,256,256]{3,0,2,1:T(8,128)}, f32[8,2,256,256]{3,0,2,1:T(8,128)}) async-done(((f32[8,2,256,256]{3,0,2,1:T(8,128)}, f32[8,2,256,256]{3,0,2,1:T(8,128)}, f32[8,2,256,256]{3,0,2,1:T(8,128)}), (f32[8,2,256,256]{3,0,2,1:T(8,128)}, f32[8,2,256,256]{3,0,2,1:T(8,128)}, f32[8,2,256,256]{3,0,2,1:T(8,128)})) %all-reduce.5.cloned.1.call-update) | async-done | bytes 12582928 | tf_op jit(solution)/shard_map/psum | solution.py:38
  264.0 8.5 %fusion.31 = (f32[8,256,256,1]{2,0,1,3:T(8,128)}, f32[8,256,256,1]{2,0,1,3:T(8,128)}, f32[8,256,256,1]{2,0,1,3:T(8,128)}, f32[8,256,256,1]{2,0,1,3:T(8,128)S(1)}...) fusion(f32[8,2,256,256]{3,0,2,1:T(8,128)} %get-tuple-element.27, f32[256,256]{1,0:T(8,128)S(1)} %fusion.78, ...), kind=kLoop, calls=%fused_computation.41 | loop fusion | flops 4718592 | bytes 25428064 | tf_op jit(solution)/shard_map/add | solution.py:22
  272.5 21.2 %fusion.22 = f32[8,256,4,256]{3,1,2,0:T(8,128)} fusion(f32[4,256,8,256]{3,2,1,0:T(8,128)} %param.11, f32[8,256,256,1]{2,0,1,3:T(8,128)S(1)} %get-tuple-element.61), kind=kOutput, calls=%fused_computation.28 | convolution fusion | flops 6442450944 | bytes 18874368 | tf_op jit(solution)/shard_map/aibm,bml->aibl/dot_general | solution.py:30
  293.8 12.7 %fusion.6 = f32[8,256,4,256]{3,1,2,0:T(8,128)} fusion(f32[8,256,4,256]{3,1,2,0:T(8,128)} %fusion.22, f32[8,256,256,1]{2,0,1,3:T(8,128)S(1)} %get-tuple-element.63), kind=kOutput, calls=%fused_computation.12 | convolution fusion | flops 6442450944 | bytes 18874368 | tf_op jit(solution)/shard_map/aibm,bml->aibl/dot_general | solution.py:30
  314.3 15.9 %fusion.24 = f32[4,256,8,256]{1,3,0,2:T(8,128)} fusion(f32[8,256,4,256]{3,1,2,0:T(8,128)} %fusion.6, f32[8,256,256,1]{2,0,1,3:T(8,128)} %get-tuple-element.45), kind=kOutput, calls=%fused_computation.30 | convolution fusion | flops 6442450944 | bytes 18874368 | tf_op jit(solution)/shard_map/aibm,bml->aibl/dot_general | solution.py:30
  330.1 10.4 %copy.155 = f32[4,256,8,256]{3,2,1,0:T(8,128)} copy(f32[4,256,8,256]{1,3,0,2:T(8,128)} %fusion.24) | data formatting | bytes 16777216
  340.5 14.8 %fusion.20 = f32[8,256,4,256]{3,1,2,0:T(8,128)S(1)} fusion(f32[8,256,256,1]{1,2,3,0:T(8,128)} %copy.163, f32[4,256,8,256]{3,2,1,0:T(8,128)} %param.12), kind=kOutput, calls=%fused_computation.26 | convolution fusion | flops 6442450944 | bytes 18874368 | tf_op jit(solution)/shard_map/aibm,bml->aibl/dot_general | solution.py:30
  355.4 8.8 %fusion.2 = f32[8,256,4,256]{3,1,2,0:T(8,128)S(1)} fusion(f32[8,256,256,1]{1,2,3,0:T(8,128)S(1)} %copy-done, f32[8,256,4,256]{3,1,2,0:T(8,128)S(1)} %fusion.20), kind=kOutput, calls=%fused_computation.8 | convolution fusion | flops 6442450944 | bytes 18874368 | tf_op jit(solution)/shard_map/aibm,bml->aibl/dot_general | solution.py:30
  364.2 9.8 %fusion.27 = f32[4,256,8,256]{1,3,0,2:T(8,128)} fusion(f32[8,256,256,1]{1,2,3,0:T(8,128)S(1)} %copy.170, f32[8,256,4,256]{3,1,2,0:T(8,128)S(1)} %fusion.2), kind=kOutput, calls=%fused_computation.31 | convolution fusion | flops 6442450944 | bytes 18874368 | tf_op jit(solution)/shard_map/aibm,bml->aibl/dot_general | solution.py:30
  374.0 10.4 %copy.156 = f32[4,256,8,256]{3,2,1,0:T(8,128)} copy(f32[4,256,8,256]{1,3,0,2:T(8,128)} %fusion.27) | data formatting | bytes 16777216
  384.4 30.7 %all-reduce.7.cloned.1.call-done = (f32[4,256,256]{2,1,0:T(8,128)}, f32[4,256,256]{2,1,0:T(8,128)}, f32[4,256,256]{2,1,0:T(8,128)}) async-done(((f32[4,256,256]{2,1,0:T(8,128)}, f32[4,256,256]{2,1,0:T(8,128)}, f32[4,256,256]{2,1,0:T(8,128)}), (f32[4,256,256]{2,1,0:T(8,128)}, f32[4,256,256]{2,1,0:T(8,128)}, f32[4,256,256]{2,1,0:T(8,128)})) %all-reduce.7.cloned.1.call-update) | async-done | bytes 3145744 | tf_op jit(solution)/shard_map/psum | solution.py:41
  415.1 14.4 %fusion.18 = f32[4,256,8,256]{3,1,0,2:T(8,128)S(1)} fusion(f32[4,256,8,256]{3,2,1,0:T(8,128)} %param.9, f32[4,256,256]{2,1,0:T(8,128)} %get-tuple-element.30, f32[4]{0:T(128)S(1)} %get-tuple-element.87, f32[256,256]{1,0:T(8,128)S(1)} %fusion.78), kind=kOutput, calls=%fused_computation.24 | convolution fusion | flops 6442975232 | bytes 18087952 | tf_op jit(solution)/shard_map/aij,aibl->ajbl/dot_general | solution.py:26
  429.5 8.9 %fusion.117 = f32[8,256,4,256]{3,1,2,0:T(8,128)S(1)} fusion(f32[8,256,256,1]{1,2,3,0:T(8,128)S(1)} %copy-done.3, f32[4,256,8,256]{3,1,0,2:T(8,128)S(1)} %fusion.18), kind=kOutput, calls=%fused_computation.194 | convolution fusion | flops 6442450944 | bytes 18874368 | tf_op jit(solution)/shard_map/aibm,bml->aibl/dot_general | solution.py:30
  438.4 14.3 %fusion.16 = f32[4,256,8,256]{3,1,0,2:T(8,128)S(1)} fusion(f32[8,256,4,256]{3,1,2,0:T(8,128)S(1)} %fusion.117, f32[4,256,256]{2,1,0:T(8,128)S(1)} %copy-done.7, f32[4]{0:T(128)S(1)} %get-tuple-element.88, f32[256,256]{1,0:T(8,128)S(1)} %fusion.78), kind=kOutput, calls=%fused_computation.22 | convolution fusion | flops 6442975232 | bytes 18087952 | tf_op jit(solution)/shard_map/aij,aibl->ajbl/dot_general | solution.py:26
  452.7 9.3 %fusion.118 = f32[8,256,4,256]{3,1,2,0:T(8,128)S(1)} fusion(f32[8,256,256,1]{1,2,3,0:T(8,128)S(1)} %copy-done.1, f32[4,256,8,256]{3,1,0,2:T(8,128)S(1)} %fusion.16), kind=kOutput, calls=%fused_computation.195 | convolution fusion | flops 6442450944 | bytes 18874368 | tf_op jit(solution)/shard_map/aibm,bml->aibl/dot_general | solution.py:30
  462.0 14.2 %fusion.14 = f32[4,256,8,256]{3,1,0,2:T(8,128)S(1)} fusion(f32[8,256,4,256]{3,1,2,0:T(8,128)S(1)} %fusion.118, f32[4,256,256]{2,1,0:T(8,128)S(1)} %copy-done.6, f32[256,256]{1,0:T(8,128)S(1)} %fusion.78, f32[4]{0:T(128)S(1)} %broadcast_subtract_fusion.2), kind=kOutput, calls=%fused_computation.20 | convolution fusion | flops 6442975232 | bytes 18087952 | tf_op jit(solution)/shard_map/aij,aibl->ajbl/dot_general | solution.py:26
  476.3 9.7 %convolution_bitcast_fusion.1 = f32[4,256,8,256]{1,3,0,2:T(8,128)} fusion(f32[8,256,256,1]{1,2,3,0:T(8,128)S(1)} %copy.170, f32[4,256,8,256]{3,1,0,2:T(8,128)S(1)} %fusion.14), kind=kOutput, calls=%fused_computation.33 | convolution fusion | flops 6442450944 | bytes 18874368 | tf_op jit(solution)/shard_map/aibm,bml->aibl/dot_general | solution.py:30
  486.0 10.4 %copy.153 = f32[4,256,8,256]{3,2,1,0:T(8,128)} copy(f32[4,256,8,256]{1,3,0,2:T(8,128)} %convolution_bitcast_fusion.1) | data formatting | bytes 16777216
  496.4 14.4 %fusion.12 = f32[4,256,8,256]{3,1,0,2:T(8,128)S(1)} fusion(f32[4,256,8,256]{3,2,1,0:T(8,128)} %param.10, f32[4,256,256]{2,1,0:T(8,128)} %get-tuple-element.30, f32[4]{0:T(128)S(1)} %get-tuple-element.87, f32[256,256]{1,0:T(8,128)S(1)} %fusion.78), kind=kOutput, calls=%fused_computation.18 | convolution fusion | flops 6442975232 | bytes 18087952 | tf_op jit(solution)/shard_map/aij,aibl->ajbl/dot_general | solution.py:26
  510.8 8.9 %fusion.119 = f32[8,256,4,256]{3,1,2,0:T(8,128)S(1)} fusion(f32[8,256,256,1]{1,2,3,0:T(8,128)S(1)} %copy-done.4, f32[4,256,8,256]{3,1,0,2:T(8,128)S(1)} %fusion.12), kind=kOutput, calls=%fused_computation.196 | convolution fusion | flops 6442450944 | bytes 18874368 | tf_op jit(solution)/shard_map/aibm,bml->aibl/dot_general | solution.py:30
  519.7 14.3 %fusion.10 = f32[4,256,8,256]{3,1,0,2:T(8,128)S(1)} fusion(f32[8,256,4,256]{3,1,2,0:T(8,128)S(1)} %fusion.119, f32[4,256,256]{2,1,0:T(8,128)S(1)} %copy-done.8, f32[4]{0:T(128)S(1)} %get-tuple-element.88, f32[256,256]{1,0:T(8,128)S(1)} %fusion.78), kind=kOutput, calls=%fused_computation.16 | convolution fusion | flops 6442975232 | bytes 18087952 | tf_op jit(solution)/shard_map/aij,aibl->ajbl/dot_general | solution.py:26
  534.0 9.3 %fusion.120 = f32[8,256,4,256]{3,1,2,0:T(8,128)S(1)} fusion(f32[8,256,256,1]{1,2,3,0:T(8,128)S(1)} %copy-done.2, f32[4,256,8,256]{3,1,0,2:T(8,128)S(1)} %fusion.10), kind=kOutput, calls=%fused_computation.197 | convolution fusion | flops 6442450944 | bytes 18874368 | tf_op jit(solution)/shard_map/aibm,bml->aibl/dot_general | solution.py:30
  543.3 14.2 %fusion.8 = f32[4,256,8,256]{3,1,0,2:T(8,128)S(1)} fusion(f32[8,256,4,256]{3,1,2,0:T(8,128)S(1)} %fusion.120, f32[4,256,256]{2,1,0:T(8,128)S(1)} %copy-done.6, f32[256,256]{1,0:T(8,128)S(1)} %fusion.78, f32[4]{0:T(128)S(1)} %broadcast_subtract_fusion.2), kind=kOutput, calls=%fused_computation.14 | convolution fusion | flops 6442975232 | bytes 18087952 | tf_op jit(solution)/shard_map/aij,aibl->ajbl/dot_general | solution.py:26
  557.5 9.7 %convolution_bitcast_fusion = f32[4,256,8,256]{1,3,0,2:T(8,128)} fusion(f32[8,256,256,1]{1,2,3,0:T(8,128)S(1)} %copy.170, f32[4,256,8,256]{3,1,0,2:T(8,128)S(1)} %fusion.8), kind=kOutput, calls=%fused_computation.32 | convolution fusion | flops 6442450944 | bytes 18874368 | tf_op jit(solution)/shard_map/aibm,bml->aibl/dot_general | solution.py:30
  567.2 10.4 %copy.154 = f32[4,256,8,256]{3,2,1,0:T(8,128)} copy(f32[4,256,8,256]{1,3,0,2:T(8,128)} %convolution_bitcast_fusion) | data formatting | bytes 16777216
  (94 shorter events, 40.9 us)
Async XLA Ops:
  7.2 3.3 copy-start.12
  7.2 246.6 %all-reduce.5.cloned.1.call-start = ((), (), s32[]{:S(2)}) async-start(), calls=%async_computation | async-start | bytes 25165824 | tf_op jit(solution)/shard_map/psum | solution.py:38
  10.3 14.5 %copy-start.13 = (s32[3,16]{1,0:T(4,128)S(1)}, s32[3,16]{1,0:T(4,128)}, u32[]{:S(2)}) copy-start(s32[3,16]{1,0:T(4,128)} %param.13) | copy-start | bytes 580
  35.3 14.7 %copy-start.9 = (f32[512,256]{1,0:T(8,128)S(1)}, f32[512,256]{1,0:T(8,128)}, u32[]{:S(2)}) copy-start(f32[512,256]{1,0:T(8,128)} %gather_fusion) | copy-start | bytes 1572868
  35.3 14.7 %copy-start.10 = (f32[512,256]{1,0:T(8,128)S(1)}, f32[512,256]{1,0:T(8,128)}, u32[]{:S(2)}) copy-start(f32[512,256]{1,0:T(8,128)} %gather_fusion.1) | copy-start | bytes 1572868
  41.8 9.4 %copy-start.11 = (f32[512,256]{1,0:T(8,128)S(1)}, f32[512,256]{1,0:T(8,128)}, u32[]{:S(2)}) copy-start(f32[512,256]{1,0:T(8,128)} %gather_fusion.3) | copy-start | bytes 1572868
  78.9 336.2 %all-reduce.7.cloned.1.call-start = ((), (), s32[]{:S(2)}) async-start(), calls=%async_computation.1 | async-start | bytes 6291456 | tf_op jit(solution)/shard_map/psum | solution.py:41
  253.8 7.9 %copy-start.5 = (f32[8,2,256,256]{3,0,2,1:T(8,128)S(1)}, f32[8,2,256,256]{3,0,2,1:T(8,128)}, u32[]{:S(2)}) copy-start(f32[8,2,256,256]{3,0,2,1:T(8,128)} %get-tuple-element.27) | copy-start | bytes 12582916
  340.5 14.8 %copy-start = (f32[8,256,256,1]{1,2,3,0:T(8,128)S(1)}, f32[8,256,256,1]{1,2,3,0:T(8,128)}, u32[]{:S(2)}) copy-start(f32[8,256,256,1]{1,2,3,0:T(8,128)} %copy.167) | copy-start | bytes 6291460
  415.1 14.4 %copy-start.3 = (f32[8,256,256,1]{1,2,3,0:T(8,128)S(1)}, f32[8,256,256,1]{1,2,3,0:T(8,128)}, u32[]{:S(2)}) copy-start(f32[8,256,256,1]{1,2,3,0:T(8,128)} %copy.163) | copy-start | bytes 6291460
  429.5 8.9 %copy-start.7 = (f32[4,256,256]{2,1,0:T(8,128)S(1)}, f32[4,256,256]{2,1,0:T(8,128)}, u32[]{:S(2)}) copy-start(f32[4,256,256]{2,1,0:T(8,128)} %get-tuple-element.31) | copy-start | bytes 3145732
  438.4 14.3 %copy-start.1 = (f32[8,256,256,1]{1,2,3,0:T(8,128)S(1)}, f32[8,256,256,1]{1,2,3,0:T(8,128)}, u32[]{:S(2)}) copy-start(f32[8,256,256,1]{1,2,3,0:T(8,128)} %copy.167) | copy-start | bytes 6291460
  452.7 9.3 %copy-start.6 = (f32[4,256,256]{2,1,0:T(8,128)S(1)}, f32[4,256,256]{2,1,0:T(8,128)}, u32[]{:S(2)}) copy-start(f32[4,256,256]{2,1,0:T(8,128)} %get-tuple-element.32) | copy-start | bytes 3145732
  496.4 14.4 %copy-start.4 = (f32[8,256,256,1]{1,2,3,0:T(8,128)S(1)}, f32[8,256,256,1]{1,2,3,0:T(8,128)}, u32[]{:S(2)}) copy-start(f32[8,256,256,1]{1,2,3,0:T(8,128)} %copy.163) | copy-start | bytes 6291460
  510.8 8.9 %copy-start.8 = (f32[4,256,256]{2,1,0:T(8,128)S(1)}, f32[4,256,256]{2,1,0:T(8,128)}, u32[]{:S(2)}) copy-start(f32[4,256,256]{2,1,0:T(8,128)} %get-tuple-element.31) | copy-start | bytes 3145732
  519.7 14.3 %copy-start.2 = (f32[8,256,256,1]{1,2,3,0:T(8,128)S(1)}, f32[8,256,256,1]{1,2,3,0:T(8,128)}, u32[]{:S(2)}) copy-start(f32[8,256,256,1]{1,2,3,0:T(8,128)} %copy.167) | copy-start | bytes 6291460
Sparse Core Ops, SparseCore 0:
  79.0 174.7 all-reduce.4
  293.9 121.1 all-reduce.6
where the time goes:
time: 594 us; the launch traced here: 585 us
  matrix products  255 us (43%)
  waiting for transfers between devices  205 us (35%)
  local copies, waits for them, and re-layouts  92.4 us (16%)
  other arithmetic  17.4 us (3%)
  between operations  14.7 us (2%)
    psum x1, waiting for transfers between devices, slot_factors(): received = lax.psum(slots, 'row')  174 us
    dot_general x12, matrix products, cols_update(): jnp.einsum('aibm,bml->aibl', matrix, factor, precision=lax.Precision.HIGH...  139 us
    dot_general x6, matrix products, rows_update(): jnp.einsum('aij,aibl->ajbl', factor, matrix, precision=lax.Precision.HIGH...  85.8 us
    unnamed x36, local copies, waits for them, and re-layouts  41.7 us
    psum x1, waiting for transfers between devices, slot_factors(): row_sum = lax.psum(row_part, 'col')  30.7 us
    dot_general x3, matrix products, slot_factors(): jnp.einsum('jw,wxab->jxab', placing, stacked, precision=lax.Precision.HIG...  23.5 us
    gather x3, local copies, waits for them, and re-layouts, window_bases(): jnp.take(factors[0], target, axis=0)  16.7 us
    gather x3, local copies, waits for them, and re-layouts, window_bases(): jnp.take(factors[1], target, axis=0)  16.6 us
  transfers between devices with their start and end apart: 2, of which 2 were waited for; matrix products, arithmetic and copies ran while one was open for 16% of the time, Pallas kernels for 0%

commit v1 on v0

--- a/solution.py
+++ b/solution.py
@@ -35,7 +35,9 @@
     stacked = jnp.stack([left_own, right_own], axis=1)
     placing = (col_blocks[:, None] == own_starts[None, :]).astype(jnp.float32)
     slots = jnp.einsum("jw,wxab->jxab", placing, stacked, precision=lax.Precision.HIGHEST)
-    received = lax.psum(slots, "row")
+    received = slots
+    for hop in (1, 2, 4):
+        received = received + lax.ppermute(received, "row", [(dev, dev ^ hop) for dev in range(8)])
     picking = (row_blocks[:, None] == col_blocks[None, :]).astype(jnp.float32)
     row_part = jnp.einsum("kj,jab->kab", picking, received[:, 0], precision=lax.Precision.HIGHEST)
     row_sum = lax.psum(row_part, "col")

time: 594 us -> 781 us (1.31)
  waiting for transfers between devices: 205 us -> 375 us
  other arithmetic: 17.4 us -> 41 us
  matrix products: 255 us -> 240 us
  starting transfers between devices: 0.08 us -> 11.9 us
    ppermute x0 -> x9, waiting for transfers between devices: none -> 343 us  [slot_factors(): lax.ppermute(received, 'row', [(dev, dev ^ hop) for dev in range(8)])]
    psum x1 -> x0, waiting for transfers between devices: 174 us -> none  [slot_factors(): received = lax.psum(slots, 'row')]
    add x0 -> x9, other arithmetic: none -> 14.3 us  [slot_factors(): received + lax.ppermute(received, 'row', [(dev, dev ^ hop) for dev in ran...]
    dot_general x3, matrix products: 23.5 us -> 11.5 us  [slot_factors(): jnp.einsum('jw,wxab->jxab', placing, stacked, precision=lax.Precision.HIG...]
    ppermute x0 -> x9, starting transfers between devices: none -> 11.8 us  [slot_factors(): lax.ppermute(received, 'row', [(dev, dev ^ hop) for dev in range(8)])]
    another operation x3, other arithmetic: 5.3 us -> 14.6 us  [slot_factors(): stacked = jnp.stack([left_own, right_own], axis=1)]
  transfers between devices with their start and end apart: 2 -> 10, of which waited for: 2 -> 5; matrix products, arithmetic and copies ran while one was open for 16% -> 19% of each run, Pallas kernels for 0% -> 0%
where the time goes in v1:
time: 781 us; the launch traced here: 771 us
  waiting for transfers between devices  375 us (48%)
  matrix products  240 us (31%)
  local copies, waits for them, and re-layouts  88.5 us (11%)
  other arithmetic  41 us (5%)
  between operations  14.8 us (2%)
  starting transfers between devices  11.9 us (2%)
    ppermute x9, waiting for transfers between devices, slot_factors(): lax.ppermute(received, 'row', [(dev, dev ^ hop) for dev in range(8)])  343 us
    dot_general x12, matrix products, cols_update(): jnp.einsum('aibm,bml->aibl', matrix, factor, precision=lax.Precision.HIGH...  139 us
    dot_general x6, matrix products, rows_update(): jnp.einsum('aij,aibl->ajbl', factor, matrix, precision=lax.Precision.HIGH...  85.8 us
    unnamed x36, local copies, waits for them, and re-layouts  42.4 us
    psum x1, waiting for transfers between devices, slot_factors(): row_sum = lax.psum(row_part, 'col')  31.8 us
  transfers between devices with their start and end apart: 10, of which 5 were waited for; matrix products, arithmetic and copies ran while one was open for 19% of the time, Pallas kernels for 0%

profile of v1, /device:TPU:0, one launch (start us, length us, event | category | flops | bytes accessed | tf_op | source)
XLA Modules:
  0.0 771.2 jit_solution(9803722542023548085)
XLA Ops:
  14.6 6.4 gather_fusion.4
  21.0 6.4 gather_fusion.5
  44.6 4.3 fusion.46
  58.5 10.4 %fusion.65 = (f32[2,1,256,256]{3,0,2,1:T(2,128)S(1)}, f32[2,1,256,256]{3,0,2,1:T(2,128)S(1)}) fusion(f32[2,256,256]{2,1,0:T(8,128)S(1)} %bitcast.246, pred[2,256]{0,1:T(8,128)(4,1)S(1)} %copy.101, f32[2,256,256]{2,1,0:T(8,128)S(1)} %bitcast.249), kind=kLoop, calls=%fused_computation.99 | loop fusion | flops 262144 | bytes 2097664 | tf_op jit(solution)/shard_map/stack | solution.py:35
  85.8 84.7 %collective-permute-done.7 = f32[8,2,256,256]{3,0,2,1:T(8,128)S(1)} collective-permute-done((f32[8,2,256,256]{3,0,2,1:T(8,128)S(1)}, f32[8,2,256,256]{3,0,2,1:T(8,128)S(1)}, u32[]{:S(2)}, u32[]{:S(2)}) %collective-permute-start.7) | collective-permute-done | bytes 4194336 | tf_op jit(solution)/shard_map/ppermute | solution.py:40
  173.1 87.2 %collective-permute-done.4 = f32[8,2,256,256]{3,0,2,1:T(8,128)S(1)} collective-permute-done((f32[8,2,256,256]{3,0,2,1:T(8,128)S(1)}, f32[8,2,256,256]{3,0,2,1:T(8,128)S(1)}, u32[]{:S(2)}, u32[]{:S(2)}) %collective-permute-start.4) | collective-permute-done | bytes 4194336 | tf_op jit(solution)/shard_map/ppermute | solution.py:40
  263.0 87.1 %collective-permute-done.1 = f32[8,2,256,256]{3,0,2,1:T(8,128)} collective-permute-done((f32[8,2,256,256]{3,0,2,1:T(8,128)S(1)}, f32[8,2,256,256]{3,0,2,1:T(8,128)}, u32[]{:S(2)}, u32[]{:S(2)}) %collective-permute-start.1) | collective-permute-done | bytes 4194336 | tf_op jit(solution)/shard_map/ppermute | solution.py:40
  361.3 84.3 %collective-permute-done.2 = f32[8,2,256,256]{3,0,2,1:T(8,128)S(1)} collective-permute-done((f32[8,2,256,256]{3,0,2,1:T(8,128)S(1)}, f32[8,2,256,256]{3,0,2,1:T(8,128)S(1)}, u32[]{:S(2)}, u32[]{:S(2)}) %collective-permute-start.2) | collective-permute-done | bytes 4194336 | tf_op jit(solution)/shard_map/ppermute | solution.py:40
  449.4 8.5 %fusion.31 = (f32[8,256,256,1]{2,0,1,3:T(8,128)}, f32[8,256,256,1]{2,0,1,3:T(8,128)}, f32[8,256,256,1]{2,0,1,3:T(8,128)}, f32[8,256,256,1]{2,0,1,3:T(8,128)S(1)}...) fusion(f32[8,2,256,256]{3,0,2,1:T(8,128)} %copy-done.7, f32[256,256]{1,0:T(8,128)S(1)} %fusion.78, ...), kind=kLoop, calls=%fused_computation.41 | loop fusion | flops 4718592 | bytes 25428064 | tf_op jit(solution)/shard_map/add | solution.py:22
  457.9 21.2 %fusion.22 = f32[8,256,4,256]{3,1,2,0:T(8,128)} fusion(f32[4,256,8,256]{3,2,1,0:T(8,128)} %param.11, f32[8,256,256,1]{2,0,1,3:T(8,128)S(1)} %get-tuple-element.58), kind=kOutput, calls=%fused_computation.28 | convolution fusion | flops 6442450944 | bytes 18874368 | tf_op jit(solution)/shard_map/aibm,bml->aibl/dot_general | solution.py:30
  479.2 12.7 %fusion.6 = f32[8,256,4,256]{3,1,2,0:T(8,128)} fusion(f32[8,256,4,256]{3,1,2,0:T(8,128)} %fusion.22, f32[8,256,256,1]{2,0,1,3:T(8,128)S(1)} %get-tuple-element.60), kind=kOutput, calls=%fused_computation.12 | convolution fusion | flops 6442450944 | bytes 18874368 | tf_op jit(solution)/shard_map/aibm,bml->aibl/dot_general | solution.py:30
  499.7 15.8 %fusion.24 = f32[4,256,8,256]{1,3,0,2:T(8,128)} fusion(f32[8,256,4,256]{3,1,2,0:T(8,128)} %fusion.6, f32[8,256,256,1]{2,0,1,3:T(8,128)} %get-tuple-element.42), kind=kOutput, calls=%fused_computation.30 | convolution fusion | flops 6442450944 | bytes 18874368 | tf_op jit(solution)/shard_map/aibm,bml->aibl/dot_general | solution.py:30
  515.5 10.4 %copy.155 = f32[4,256,8,256]{3,2,1,0:T(8,128)} copy(f32[4,256,8,256]{1,3,0,2:T(8,128)} %fusion.24) | data formatting | bytes 16777216
  526.0 14.8 %fusion.20 = f32[8,256,4,256]{3,1,2,0:T(8,128)S(1)} fusion(f32[8,256,256,1]{1,2,3,0:T(8,128)} %copy.163, f32[4,256,8,256]{3,2,1,0:T(8,128)} %param.12), kind=kOutput, calls=%fused_computation.26 | convolution fusion | flops 6442450944 | bytes 18874368 | tf_op jit(solution)/shard_map/aibm,bml->aibl/dot_general | solution.py:30
  540.7 8.8 %fusion.2 = f32[8,256,4,256]{3,1,2,0:T(8,128)S(1)} fusion(f32[8,256,256,1]{1,2,3,0:T(8,128)S(1)} %copy-done, f32[8,256,4,256]{3,1,2,0:T(8,128)S(1)} %fusion.20), kind=kOutput, calls=%fused_computation.8 | convolution fusion | flops 6442450944 | bytes 18874368 | tf_op jit(solution)/shard_map/aibm,bml->aibl/dot_general | solution.py:30
  549.6 9.8 %fusion.27 = f32[4,256,8,256]{1,3,0,2:T(8,128)} fusion(f32[8,256,256,1]{1,2,3,0:T(8,128)S(1)} %copy.170, f32[8,256,4,256]{3,1,2,0:T(8,128)S(1)} %fusion.2), kind=kOutput, calls=%fused_computation.31 | convolution fusion | flops 6442450944 | bytes 18874368 | tf_op jit(solution)/shard_map/aibm,bml->aibl/dot_general | solution.py:30
  559.4 10.4 %copy.156 = f32[4,256,8,256]{3,2,1,0:T(8,128)} copy(f32[4,256,8,256]{1,3,0,2:T(8,128)} %fusion.27) | data formatting | bytes 16777216
  569.8 31.8 %all-reduce.3.cloned.1.call-done = (f32[4,256,256]{2,1,0:T(8,128)}, f32[4,256,256]{2,1,0:T(8,128)}, f32[4,256,256]{2,1,0:T(8,128)}) async-done(((f32[4,256,256]{2,1,0:T(8,128)}, f32[4,256,256]{2,1,0:T(8,128)}, f32[4,256,256]{2,1,0:T(8,128)}), (f32[4,256,256]{2,1,0:T(8,128)}, f32[4,256,256]{2,1,0:T(8,128)}, f32[4,256,256]{2,1,0:T(8,128)})) %all-reduce.3.cloned.1.call-update) | async-done | bytes 3145744 | tf_op jit(solution)/shard_map/psum | solution.py:43
  601.6 14.4 %fusion.18 = f32[4,256,8,256]{3,1,0,2:T(8,128)S(1)} fusion(f32[4,256,8,256]{3,2,1,0:T(8,128)} %param.9, f32[4,256,256]{2,1,0:T(8,128)} %get-tuple-element.27, f32[4]{0:T(128)S(1)} %get-tuple-element.82, f32[256,256]{1,0:T(8,128)S(1)} %fusion.78), kind=kOutput, calls=%fused_computation.24 | convolution fusion | flops 6442975232 | bytes 18087952 | tf_op jit(solution)/shard_map/aij,aibl->ajbl/dot_general | solution.py:26
  616.1 8.9 %fusion.118 = f32[8,256,4,256]{3,1,2,0:T(8,128)S(1)} fusion(f32[8,256,256,1]{1,2,3,0:T(8,128)S(1)} %copy-done.3, f32[4,256,8,256]{3,1,0,2:T(8,128)S(1)} %fusion.18), kind=kOutput, calls=%fused_computation.195 | convolution fusion | flops 6442450944 | bytes 18874368 | tf_op jit(solution)/shard_map/aibm,bml->aibl/dot_general | solution.py:30
  625.0 14.3 %fusion.16 = f32[4,256,8,256]{3,1,0,2:T(8,128)S(1)} fusion(f32[8,256,4,256]{3,1,2,0:T(8,128)S(1)} %fusion.118, f32[4,256,256]{2,1,0:T(8,128)S(1)} %copy-done.9, f32[4]{0:T(128)S(1)} %get-tuple-element.83, f32[256,256]{1,0:T(8,128)S(1)} %fusion.78), kind=kOutput, calls=%fused_computation.22 | convolution fusion | flops 6442975232 | bytes 18087952 | tf_op jit(solution)/shard_map/aij,aibl->ajbl/dot_general | solution.py:26
  639.3 9.3 %fusion.119 = f32[8,256,4,256]{3,1,2,0:T(8,128)S(1)} fusion(f32[8,256,256,1]{1,2,3,0:T(8,128)S(1)} %copy-done.1, f32[4,256,8,256]{3,1,0,2:T(8,128)S(1)} %fusion.16), kind=kOutput, calls=%fused_computation.196 | convolution fusion | flops 6442450944 | bytes 18874368 | tf_op jit(solution)/shard_map/aibm,bml->aibl/dot_general | solution.py:30
  648.6 14.2 %fusion.14 = f32[4,256,8,256]{3,1,0,2:T(8,128)S(1)} fusion(f32[8,256,4,256]{3,1,2,0:T(8,128)S(1)} %fusion.119, f32[4,256,256]{2,1,0:T(8,128)S(1)} %copy-done.8, f32[256,256]{1,0:T(8,128)S(1)} %fusion.78, f32[4]{0:T(128)S(1)} %broadcast_subtract_fusion.2), kind=kOutput, calls=%fused_computation.20 | convolution fusion | flops 6442975232 | bytes 18087952 | tf_op jit(solution)/shard_map/aij,aibl->ajbl/dot_general | solution.py:26
  662.8 9.7 %convolution_bitcast_fusion.1 = f32[4,256,8,256]{1,3,0,2:T(8,128)} fusion(f32[8,256,256,1]{1,2,3,0:T(8,128)S(1)} %copy.170, f32[4,256,8,256]{3,1,0,2:T(8,128)S(1)} %fusion.14), kind=kOutput, calls=%fused_computation.33 | convolution fusion | flops 6442450944 | bytes 18874368 | tf_op jit(solution)/shard_map/aibm,bml->aibl/dot_general | solution.py:30
  672.5 10.4 %copy.153 = f32[4,256,8,256]{3,2,1,0:T(8,128)} copy(f32[4,256,8,256]{1,3,0,2:T(8,128)} %convolution_bitcast_fusion.1) | data formatting | bytes 16777216
  682.9 14.4 %fusion.12 = f32[4,256,8,256]{3,1,0,2:T(8,128)S(1)} fusion(f32[4,256,8,256]{3,2,1,0:T(8,128)} %param.10, f32[4,256,256]{2,1,0:T(8,128)} %get-tuple-element.27, f32[4]{0:T(128)S(1)} %get-tuple-element.82, f32[256,256]{1,0:T(8,128)S(1)} %fusion.78), kind=kOutput, calls=%fused_computation.18 | convolution fusion | flops 6442975232 | bytes 18087952 | tf_op jit(solution)/shard_map/aij,aibl->ajbl/dot_general | solution.py:26
  697.4 8.9 %fusion.120 = f32[8,256,4,256]{3,1,2,0:T(8,128)S(1)} fusion(f32[8,256,256,1]{1,2,3,0:T(8,128)S(1)} %copy-done.4, f32[4,256,8,256]{3,1,0,2:T(8,128)S(1)} %fusion.12), kind=kOutput, calls=%fused_computation.197 | convolution fusion | flops 6442450944 | bytes 18874368 | tf_op jit(solution)/shard_map/aibm,bml->aibl/dot_general | solution.py:30
  706.3 14.3 %fusion.10 = f32[4,256,8,256]{3,1,0,2:T(8,128)S(1)} fusion(f32[8,256,4,256]{3,1,2,0:T(8,128)S(1)} %fusion.120, f32[4,256,256]{2,1,0:T(8,128)S(1)} %copy-done.10, f32[4]{0:T(128)S(1)} %get-tuple-element.83, f32[256,256]{1,0:T(8,128)S(1)} %fusion.78), kind=kOutput, calls=%fused_computation.16 | convolution fusion | flops 6442975232 | bytes 18087952 | tf_op jit(solution)/shard_map/aij,aibl->ajbl/dot_general | solution.py:26
  720.5 9.3 %fusion.121 = f32[8,256,4,256]{3,1,2,0:T(8,128)S(1)} fusion(f32[8,256,256,1]{1,2,3,0:T(8,128)S(1)} %copy-done.2, f32[4,256,8,256]{3,1,0,2:T(8,128)S(1)} %fusion.10), kind=kOutput, calls=%fused_computation.198 | convolution fusion | flops 6442450944 | bytes 18874368 | tf_op jit(solution)/shard_map/aibm,bml->aibl/dot_general | solution.py:30
  729.8 14.2 %fusion.8 = f32[4,256,8,256]{3,1,0,2:T(8,128)S(1)} fusion(f32[8,256,4,256]{3,1,2,0:T(8,128)S(1)} %fusion.121, f32[4,256,256]{2,1,0:T(8,128)S(1)} %copy-done.8, f32[256,256]{1,0:T(8,128)S(1)} %fusion.78, f32[4]{0:T(128)S(1)} %broadcast_subtract_fusion.2), kind=kOutput, calls=%fused_computation.14 | convolution fusion | flops 6442975232 | bytes 18087952 | tf_op jit(solution)/shard_map/aij,aibl->ajbl/dot_general | solution.py:26
  744.1 9.7 %convolution_bitcast_fusion = f32[4,256,8,256]{1,3,0,2:T(8,128)} fusion(f32[8,256,256,1]{1,2,3,0:T(8,128)S(1)} %copy.170, f32[4,256,8,256]{3,1,0,2:T(8,128)S(1)} %fusion.8), kind=kOutput, calls=%fused_computation.32 | convolution fusion | flops 6442450944 | bytes 18874368 | tf_op jit(solution)/shard_map/aibm,bml->aibl/dot_general | solution.py:30
  753.8 10.4 %copy.154 = f32[4,256,8,256]{3,2,1,0:T(8,128)} copy(f32[4,256,8,256]{1,3,0,2:T(8,128)} %convolution_bitcast_fusion) | data formatting | bytes 16777216
  (119 shorter events, 79.0 us)
Async XLA Ops:
  7.2 3.2 copy-start.12
  7.2 3.2 copy-start.13
  7.2 594.4 %all-reduce.3.cloned.1.call-start = ((), (), s32[]{:S(2)}) async-start(), calls=%async_computation | async-start | bytes 6291456 | tf_op jit(solution)/shard_map/psum | solution.py:43
  21.0 6.4 copy-start.11
  34.7 37.7 %collective-permute-start.6 = (f32[8,2,256,256]{3,0,2,1:T(8,128)}, f32[8,2,256,256]{3,0,2,1:T(8,128)}, u32[]{:S(2)}, u32[]{:S(2)}) collective-permute-start(f32[8,2,256,256]{3,0,2,1:T(8,128)} %fusion.50), channel_id=1, source_target_pairs={{0,4},{4,0},{8,12},{12,8},{16,20},{20,16},{24,28},{28,24},{1,5},{5... | collective-permute-start | bytes 12582920 | tf_op jit(solution)/shard_map/ppermute | solution.py:40
  48.9 30.1 %collective-permute-start.3 = (f32[8,2,256,256]{3,0,2,1:T(8,128)}, f32[8,2,256,256]{3,0,2,1:T(8,128)}, u32[]{:S(2)}, u32[]{:S(2)}) collective-permute-start(f32[8,2,256,256]{3,0,2,1:T(8,128)} %fusion.46), channel_id=1, source_target_pairs={{0,4},{4,0},{8,12},{12,8},{16,20},{20,16},{24,28},{28,24},{1,5},{5... | collective-permute-start | bytes 12582920 | tf_op jit(solution)/shard_map/ppermute | solution.py:40
  71.9 11.3 %collective-permute-start = (f32[8,2,256,256]{3,0,2,1:T(8,128)S(1)}, f32[8,2,256,256]{3,0,2,1:T(8,128)S(1)}, u32[]{:S(2)}, u32[]{:S(2)}) collective-permute-start(f32[8,2,256,256]{3,0,2,1:T(8,128)S(1)} %fusion.42), channel_id=1, source_target_pairs={{0,4},{4,0},{8,12},{12,8},{16,20},{20,16},{24,28},{28,24},{1,5},{5... | collective-permute-start | bytes 12582920 | tf_op jit(solution)/shard_map/ppermute | solution.py:40
  76.4 94.0 %collective-permute-start.7 = (f32[8,2,256,256]{3,0,2,1:T(8,128)S(1)}, f32[8,2,256,256]{3,0,2,1:T(8,128)S(1)}, u32[]{:S(2)}, u32[]{:S(2)}) collective-permute-start(f32[8,2,256,256]{3,0,2,1:T(8,128)S(1)} %add.161), channel_id=1, source_target_pairs={{0,8},{4,12},{8,0},{12,4},{16,24},{20,28},{24,16},{28,20},{1,9},{5... | collective-permute-start | bytes 12582920 | tf_op jit(solution)/shard_map/ppermute | solution.py:40
  83.0 177.3 %collective-permute-start.4 = (f32[8,2,256,256]{3,0,2,1:T(8,128)S(1)}, f32[8,2,256,256]{3,0,2,1:T(8,128)S(1)}, u32[]{:S(2)}, u32[]{:S(2)}) collective-permute-start(f32[8,2,256,256]{3,0,2,1:T(8,128)S(1)} %add.153), channel_id=1, source_target_pairs={{0,8},{4,12},{8,0},{12,4},{16,24},{20,28},{24,16},{28,20},{1,9},{5... | collective-permute-start | bytes 12582920 | tf_op jit(solution)/shard_map/ppermute | solution.py:40
  83.7 266.4 %collective-permute-start.1 = (f32[8,2,256,256]{3,0,2,1:T(8,128)S(1)}, f32[8,2,256,256]{3,0,2,1:T(8,128)}, u32[]{:S(2)}, u32[]{:S(2)}) collective-permute-start(f32[8,2,256,256]{3,0,2,1:T(8,128)S(1)} %add.143), channel_id=1, source_target_pairs={{0,8},{4,12},{8,0},{12,4},{16,24},{20,28},{24,16},{28,20},{1,9},{5... | collective-permute-start | bytes 12582920 | tf_op jit(solution)/shard_map/ppermute | solution.py:40
  171.0 184.4 %collective-permute-start.8 = (f32[8,2,256,256]{3,0,2,1:T(8,128)S(1)}, f32[8,2,256,256]{3,0,2,1:T(8,128)S(1)}, u32[]{:S(2)}, u32[]{:S(2)}) collective-permute-start(f32[8,2,256,256]{3,0,2,1:T(8,128)S(1)} %add.162), channel_id=1, source_target_pairs={{0,16},{4,20},{8,24},{12,28},{16,0},{20,4},{24,8},{28,12},{1,17},{... | collective-permute-start | bytes 12582920 | tf_op jit(solution)/shard_map/ppermute | solution.py:40
  260.9 97.5 %collective-permute-start.5 = (f32[8,2,256,256]{3,0,2,1:T(8,128)S(1)}, f32[8,2,256,256]{3,0,2,1:T(8,128)S(1)}, u32[]{:S(2)}, u32[]{:S(2)}) collective-permute-start(f32[8,2,256,256]{3,0,2,1:T(8,128)S(1)} %add.154), channel_id=1, source_target_pairs={{0,16},{4,20},{8,24},{12,28},{16,0},{20,4},{24,8},{28,12},{1,17},{... | collective-permute-start | bytes 12582920 | tf_op jit(solution)/shard_map/ppermute | solution.py:40
  353.1 92.4 %collective-permute-start.2 = (f32[8,2,256,256]{3,0,2,1:T(8,128)S(1)}, f32[8,2,256,256]{3,0,2,1:T(8,128)S(1)}, u32[]{:S(2)}, u32[]{:S(2)}) collective-permute-start(f32[8,2,256,256]{3,0,2,1:T(8,128)S(1)} %add.144), channel_id=1, source_target_pairs={{0,16},{4,20},{8,24},{12,28},{16,0},{20,4},{24,8},{28,12},{1,17},{... | collective-permute-start | bytes 12582920 | tf_op jit(solution)/shard_map/ppermute | solution.py:40
  355.9 3.0 copy-start.5
  358.9 87.2 %copy-start.6 = (f32[8,2,256,256]{3,0,2,1:T(8,128)}, f32[8,2,256,256]{3,0,2,1:T(8,128)S(1)}, u32[]{:S(2)}) copy-start(f32[8,2,256,256]{3,0,2,1:T(8,128)S(1)} %add.155) | copy-start | bytes 12582916
  446.1 2.0 copy-start.7
  526.0 14.8 %copy-start = (f32[8,256,256,1]{1,2,3,0:T(8,128)S(1)}, f32[8,256,256,1]{1,2,3,0:T(8,128)}, u32[]{:S(2)}) copy-start(f32[8,256,256,1]{1,2,3,0:T(8,128)} %copy.167) | copy-start | bytes 6291460
  601.6 14.4 %copy-start.3 = (f32[8,256,256,1]{1,2,3,0:T(8,128)S(1)}, f32[8,256,256,1]{1,2,3,0:T(8,128)}, u32[]{:S(2)}) copy-start(f32[8,256,256,1]{1,2,3,0:T(8,128)} %copy.163) | copy-start | bytes 6291460
  616.0 8.9 %copy-start.9 = (f32[4,256,256]{2,1,0:T(8,128)S(1)}, f32[4,256,256]{2,1,0:T(8,128)}, u32[]{:S(2)}) copy-start(f32[4,256,256]{2,1,0:T(8,128)} %get-tuple-element.28) | copy-start | bytes 3145732
  625.0 14.3 %copy-start.1 = (f32[8,256,256,1]{1,2,3,0:T(8,128)S(1)}, f32[8,256,256,1]{1,2,3,0:T(8,128)}, u32[]{:S(2)}) copy-start(f32[8,256,256,1]{1,2,3,0:T(8,128)} %copy.167) | copy-start | bytes 6291460
  639.2 9.3 %copy-start.8 = (f32[4,256,256]{2,1,0:T(8,128)S(1)}, f32[4,256,256]{2,1,0:T(8,128)}, u32[]{:S(2)}) copy-start(f32[4,256,256]{2,1,0:T(8,128)} %get-tuple-element.29) | copy-start | bytes 3145732
  682.9 14.4 %copy-start.4 = (f32[8,256,256,1]{1,2,3,0:T(8,128)S(1)}, f32[8,256,256,1]{1,2,3,0:T(8,128)}, u32[]{:S(2)}) copy-start(f32[8,256,256,1]{1,2,3,0:T(8,128)} %copy.163) | copy-start | bytes 6291460
  697.3 8.9 %copy-start.10 = (f32[4,256,256]{2,1,0:T(8,128)S(1)}, f32[4,256,256]{2,1,0:T(8,128)}, u32[]{:S(2)}) copy-start(f32[4,256,256]{2,1,0:T(8,128)} %get-tuple-element.28) | copy-start | bytes 3145732
  706.3 14.3 %copy-start.2 = (f32[8,256,256,1]{1,2,3,0:T(8,128)S(1)}, f32[8,256,256,1]{1,2,3,0:T(8,128)}, u32[]{:S(2)}) copy-start(f32[8,256,256,1]{1,2,3,0:T(8,128)} %copy.167) | copy-start | bytes 6291460
Sparse Core Ops, SparseCore 0:
  479.3 122.2 all-reduce.2
